TPU v7x, 512 devices: a whole 4x8x8 slice. The times are simulated.
512 devices in a mesh: cons: 4 (over y_hi), ty: 8 (over x, y_lo), tx: 16 (over z, core).
Axes of the slice: x: 4, y: 8 (y_hi: 4, y_lo: 2; y = y_hi * 2 + y_lo), z: 8, core: 2. Of those that a mesh axis runs over, the one named last changes fastest.
Arguments:
- elevation: float32 [8, 2, 1152, 8192], P('cons', None, 'ty', 'tx'), may hold values from -6 to 6
- equilibrium: float32 [8, 2, 1152, 8192], P('cons', None, 'ty', 'tx'), may hold values from -5 to 5
- depth: float32 [1152, 8192], P('ty', 'tx'), may hold values from 0.1 to 1
- land_mask: int32 [1152, 8192], P('ty', 'tx'), may hold values 0 or 1
- friction_prev: float32 [1152, 8192], P('ty', 'tx'), may hold values from 0.3 to 3
Outputs:
- elevation_out: float32 [8, 2, 1152, 8192], P('cons', None, 'ty', 'tx')
- friction: float32 [1152, 8192], P('ty', 'tx')
All inputs are finite; a program needn't handle non-finite values. No bound on the sum of `land_mask` on one device may be relied on, other than what follows from the above.
Results may differ from a plain program's by a relative error of at most 0.00002.
Values sent between devices are 32-bit elements; how exact they have to be, the bound alone decides.
A program may use at most 64 MiB of HBM per device.

v0:
```python
import math
import jax
import jax.numpy as jnp
from jax import lax
from jax.sharding import PartitionSpec as P

OMEGA_TABLE = (1.0, 1.0351, 0.9582, 1.0379, 0.5181, 0.4816, 0.5164, 0.4454)
AY_SCALE = 0.5
THETA = 0.05
DRAG = 0.5
BACKGROUND = 0.01


def passed_along(value, axis, steps):
    count = lax.axis_size(axis)
    pairs = [(source, (source + steps) % count) for source in range(count)]
    return lax.ppermute(value, axis, pairs)


def passed_along_2(block, axis, distance):
    devices = range(lax.axis_size(axis))
    route = [(i - distance, i) for i in devices if i - distance in devices]
    return lax.ppermute(block, axis, route)


def latitude_factor(rows, total):
    lat = (-60.0 + 120.0 * (rows.astype(jnp.float32) + 0.5) / total) * (math.pi / 180.0)
    return 0.5 / jnp.cos(lat)


def momentum(num_re, num_im, fric, omega, face_mask):
    denom = fric * fric + omega * omega
    return (
        face_mask * (num_re * fric + num_im * omega) / denom,
        face_mask * (num_im * fric - num_re * omega) / denom,
    )


def ahead_rims(planes):
    east_col = passed_along(planes[:, :, 0], "tx", -1)
    north_row = passed_along_2(planes[:, 0, :], "ty", -1)
    return (east_col, north_row)


def forward_rims(planes):
    east_col, north_row = ahead_rims(planes)
    east_view = jnp.concatenate([planes[:, :, 1:], east_col[:, :, None]], axis=2)
    north_view = jnp.concatenate([planes[:, 1:, :], north_row[:, None, :]], axis=1)
    return (east_view, north_view)


def backward_rims(trans_u, trans_v):
    west_col = passed_along(trans_u[..., :, -1], "tx", 1)
    south_row = passed_along_2(trans_v[..., -1, :], "ty", 1)
    west_u = jnp.concatenate([west_col[..., None], trans_u[..., :, :-1]], axis=-1)
    south_v = jnp.concatenate([south_row[..., None, :], trans_v[..., :-1, :]], axis=-2)
    return (west_u, south_v)


def finish(eta, trans_u, west_u, trans_v, south_v, omega, ax_rows, maskf, depth):
    div = ax_rows * (trans_u - west_u) + AY_SCALE * (trans_v - south_v)
    res = jnp.stack([-omega * eta[:, 1] + div[:, 0], omega * eta[:, 0] + div[:, 1]], axis=1)
    eta_new = maskf * (eta - THETA * res)
    cu = 0.5 * (trans_u + west_u)
    cv = 0.5 * (trans_v + south_v)
    term = 0.5 * (
        cu[:, 0] * cu[:, 0] + cu[:, 1] * cu[:, 1] + cv[:, 0] * cv[:, 0] + cv[:, 1] * cv[:, 1]
    )
    variance_part = jnp.sum(term, axis=0) / (depth * depth)
    return (eta_new, variance_part)


def sweep_core(eta, zeta, zeta_east, zeta_north, fric, fric_east, fric_north, omega, statics):
    ax_rows, maskf, mu_face, mv_face, hu_face, hv_face, depth = statics
    grad_x = ax_rows * (zeta_east - zeta)
    grad_y = AY_SCALE * (zeta_north - zeta)
    fric_u = 0.5 * (fric + fric_east)
    fric_v = 0.5 * (fric + fric_north)
    u_re, u_im = momentum(-hu_face * grad_x[:, 0], -hu_face * grad_x[:, 1], fric_u, omega, mu_face)
    v_re, v_im = momentum(-hv_face * grad_y[:, 0], -hv_face * grad_y[:, 1], fric_v, omega, mv_face)
    trans_u = jnp.stack([u_re, u_im], axis=1)
    trans_v = jnp.stack([v_re, v_im], axis=1)
    west_u, south_v = backward_rims(trans_u, trans_v)
    return finish(eta, trans_u, west_u, trans_v, south_v, omega, ax_rows, maskf, depth)


def compute_friction(variance_local, depth):
    variance_total = lax.psum(variance_local, "cons")
    return DRAG * jnp.sqrt(variance_total + BACKGROUND) / depth


def body(elevation, equilibrium, depth, land_mask, friction_prev):
    kdev, two, rows_dev, cols_dev = elevation.shape
    first_cons = lax.axis_index("cons") * kdev
    omega = lax.dynamic_slice_in_dim(jnp.array(OMEGA_TABLE, dtype=jnp.float32), first_cons, kdev)[
        :, None, None
    ]
    rows = lax.axis_index("ty") * rows_dev + jnp.arange(rows_dev, dtype=jnp.int32)
    ax_rows = latitude_factor(rows, rows_dev * lax.axis_size("ty"))[:, None]
    maskf = land_mask.astype(jnp.float32)
    planes_count = kdev * 2
    zeta = elevation - equilibrium
    planes = jnp.concatenate(
        [
            zeta.reshape(planes_count, rows_dev, cols_dev),
            friction_prev[None],
            depth[None],
            maskf[None],
        ],
        axis=0,
    )
    east_view, north_view = forward_rims(planes)
    depth_east = east_view[planes_count + 1]
    depth_north = north_view[planes_count + 1]
    mask_east = east_view[planes_count + 2]
    mask_north = north_view[planes_count + 2]
    statics = (
        ax_rows,
        maskf,
        maskf * mask_east,
        maskf * mask_north,
        0.5 * (depth + depth_east),
        0.5 * (depth + depth_north),
        depth,
    )
    eta_one, variance_local = sweep_core(
        elevation,
        zeta,
        east_view[:planes_count].reshape(kdev, 2, rows_dev, cols_dev),
        north_view[:planes_count].reshape(kdev, 2, rows_dev, cols_dev),
        friction_prev,
        east_view[planes_count],
        north_view[planes_count],
        omega,
        statics,
    )
    friction = compute_friction(variance_local, depth)
    zeta_two = eta_one - equilibrium
    planes_two = jnp.concatenate(
        [zeta_two.reshape(planes_count, rows_dev, cols_dev), friction[None]], axis=0
    )
    east_two, north_two = forward_rims(planes_two)
    eta_two, unused = sweep_core(
        eta_one,
        zeta_two,
        east_two[:planes_count].reshape(kdev, 2, rows_dev, cols_dev),
        north_two[:planes_count].reshape(kdev, 2, rows_dev, cols_dev),
        friction,
        east_two[planes_count],
        north_two[planes_count],
        omega,
        statics,
    )
    return (eta_two, friction)


def solution(mesh):
    return jax.shard_map(
        body,
        mesh=mesh,
        in_specs=(
            P("cons", None, "ty", "tx"),
            P("cons", None, "ty", "tx"),
            P("ty", "tx"),
            P("ty", "tx"),
            P("ty", "tx"),
        ),
        out_specs=(P("cons", None, "ty", "tx"), P("ty", "tx")),
        check_vma=False,
    )
```

profile of v0, /device:TPU:1, one launch (start us, length us, event | category | flops | bytes accessed | tf_op | source)
XLA Modules:
  0.0 136.4 jit_solution(13368709324180972753)
XLA Ops:
  7.2 1.7 %fusion.62 = (f32[144,512]{1,0:T(8,128)}, f32[1,144,512]{2,1,0:T(8,128)S(1)}) fusion(s32[144,512]{1,0:T(8,128)} %param.9), kind=kLoop, calls=%fused_computation.150 | loop fusion | flops 73728 | bytes 884736 | tf_op jit(solution)/shard_map/convert_element_type | solution.py:100
  8.9 1.9 %sub.52 = f32[2,2,144,512]{3,2,1,0:T(8,128)S(1)} subtract(f32[2,2,144,512]{3,2,1,0:T(8,128)} %param.6, f32[2,2,144,512]{3,2,1,0:T(8,128)} %param.7) | non-fusion elementwise | flops 294912 | bytes 3538944 | tf_op jit(solution)/shard_map/sub | solution.py:102
  10.9 1.3 collective-permute-start.2
  13.3 6.9 %collective-permute-start = (f32[7,144]{1,0:T(8,128)}, f32[7,144]{1,0:T(8,128)}, u32[]{:S(2)}, u32[]{:S(2)}) collective-permute-start(f32[7,144]{1,0:T(8,128)} %slice_reduce_fusion), channel_id=1, source_target_pairs={{0,15},{1,0},{2,1},{3,2},{4,3},{5,4},{6,5},{7,6},{8,7},{9,8},{10,9... | collective-permute-start | bytes 12104 | tf_op jit(solution)/shard_map/ppermute | solution.py:17
  20.2 1.3 dynamic-slice_negate_fusion
  22.1 1.8 %slice.206 = f32[7,143,512]{2,1,0:T(8,128)} slice(f32[7,144,512]{2,1,0:T(8,128)S(1)} %pad_maximum_fusion), slice={[0:7], [1:144], [0:512]} | slice | bytes 4100096 | tf_op jit(solution)/shard_map/slice | solution.py:48
  23.9 1.9 %slice.196 = f32[7,144,511]{2,1,0:T(8,128)} slice(f32[7,144,512]{2,1,0:T(8,128)S(1)} %pad_maximum_fusion), slice={[0:7], [0:144], [1:512]} | slice | bytes 4120704 | tf_op jit(solution)/shard_map/slice | solution.py:47
  25.8 1.9 %copy.28 = f32[7,144,1]{2,1,0:T(8,128)} copy(f32[7,144,1]{1,0,2:T(8,128)} %bitcast.4) | data formatting | bytes 8064 | tf_op jit(solution)/shard_map/broadcast_in_dim | solution.py:47
  27.6 1.6 %fusion.14 = f32[4,144,512]{2,1,0:T(8,128)S(1)} fusion(f32[7,144,511]{2,1,0:T(8,128)} %slice.196, f32[7,144,1]{2,1,0:T(8,128)} %copy.28), kind=kLoop, calls=%fused_computation.49 | loop fusion | flops 294912 | bytes 3244032 | tf_op jit(solution)/shard_map/concatenate | solution.py:47
  30.0 1.5 %fusion.60 = (f32[144,512]{1,0:T(8,128)S(1)}, f32[144,512]{1,0:T(8,128)S(1)}, f32[144,512]{1,0:T(8,128)S(1)}, f32[144,512]{1,0:T(8,128)S(1)}, f32[144,512]{1,0:T...) fusion(f32[144,512]{1,0:T(8,128)} %param.10, ...), kind=kLoop, calls=%fused_computation.149 | loop fusion | flops 1548288 | bytes 7372800 | tf_op jit(solution)/shard_map/mul | solution.py:32
  35.1 4.3 %collective-permute-start.3 = (f32[2,2,512]{2,1,0:T(2,128)S(1)}, f32[2,2,512]{2,1,0:T(2,128)S(1)}, u32[]{:S(2)}, u32[]{:S(2)}) collective-permute-start(f32[2,2,512]{2,1,0:T(2,128)S(1)} %bitcast.102), channel_id=1, source_target_pairs={{0,16},{16,32},{32,48},{48,64},{64,80},{80,96},{96,112},{1,17},{17... | collective-permute-start | bytes 24584 | tf_op jit(solution)/shard_map/ppermute | solution.py:23
  40.7 3.4 %add_multiply_fusion.1 = (f32[2,2,144,512]{3,2,1,0:T(8,128)S(1)}, f32[2,2,144,512]{3,2,1,0:T(8,128)}, f32[2,2,144,512]{3,2,1,0:T(8,128)S(1)}) fusion(f32[2,1,144,512]{3,2,1,0:T(8,128)S(1)} %get-tuple-element.22, f32[2,1,144,512]{3,2,1,0:T(8,128)S(1)} %get-tuple-element.21, f32[2,2,144,511]{3,2,1,0:T(8,128)} %fusion.12, f32[2,2,144,1]{3,2,1,0:T(8,128)S(1)} %copy.29, ...), kind=kLoop, calls=%fused_computation.61 | loop fusion | flops 3833856 | bytes 8258112 | tf_op jit(solution)/shard_map/mul | solution.py:64
  47.2 1.5 %fusion.56 = (f32[2,2,144,512]{3,2,1,0:T(8,128)S(1)}, f32[2,2,144,512]{3,2,1,0:T(8,128)}) fusion(f32[2,2,144,512]{3,2,1,0:T(8,128)S(1)} %copy-done.7, f32[2,2,144,512]{3,2,1,0:T(8,128)S(1)} %copy-done.4, f32[2,1,144,512]{3,2,1,0:T(8,128)S(1)} %get-tuple-element.28, f32[2,1,144,512]{3,2,1,0:T(8,128)S(1)} %get-tuple-element.27, f32[144,512]{1,0:T(8,128)S(1)} %copy-done.10), kind=kLoop, calls=%fused_computation.147 | loop fusion | flops 1474560 | bytes 6193152 | tf_op jit(solution)/shard_map/sub | solution.py:138
  48.7 52.7 %all-reduce.2.cloned.1.call-done = f32[144,512]{1,0:T(8,128)} async-done(((f32[144,512]{1,0:T(8,128)}), f32[144,512]{1,0:T(8,128)}) %all-reduce.2.cloned.1.call-update) | async-done | bytes 294928 | tf_op jit(solution)/shard_map/psum | solution.py:88
  102.7 1.6 %fusion.1 = f32[5,144,511]{2,1,0:T(8,128)} fusion(f32[4,144,512]{2,1,0:T(8,128)S(1)} %bitcast.82, f32[1,144,512]{2,1,0:T(8,128)S(1)} %bitcast.88), kind=kLoop, calls=%fused_computation.32 | loop fusion | flops 367920 | bytes 2946240 | tf_op jit(solution)/shard_map/concatenate | solution.py:139
  104.6 2.7 %collective-permute-start.4 = (f32[5,144]{1,0:T(8,128)S(1)}, f32[5,144]{1,0:T(8,128)S(1)}, u32[]{:S(2)}, u32[]{:S(2)}) collective-permute-start(f32[5,144]{1,0:T(8,128)S(1)} %fusion.25), channel_id=1, source_target_pairs={{0,15},{1,0},{2,1},{3,2},{4,3},{5,4},{6,5},{7,6},{8,7},{9,8},{10,9... | collective-permute-start | bytes 8648 | tf_op jit(solution)/shard_map/ppermute | solution.py:17
  107.3 1.3 collective-permute-start.6
  108.6 1.3 collective-permute-done.4
  110.0 1.5 %fusion.3 = f32[4,144,512]{2,1,0:T(8,128)S(1)} fusion(f32[5,144,511]{2,1,0:T(8,128)} %fusion.1, f32[5,144,1]{2,1,0:T(8,128)S(1)} %copy.31), kind=kLoop, calls=%fused_computation.38 | loop fusion | flops 294912 | bytes 2654208 | tf_op jit(solution)/shard_map/concatenate | solution.py:47
  114.6 2.5 %collective-permute-start.5 = (f32[2,2,144]{2,1,0:T(2,128)S(1)}, f32[2,2,144]{2,1,0:T(2,128)S(1)}, u32[]{:S(2)}, u32[]{:S(2)}) collective-permute-start(f32[2,2,144]{2,1,0:T(2,128)S(1)} %fusion.27), channel_id=1, source_target_pairs={{0,1},{1,2},{2,3},{3,4},{4,5},{5,6},{6,7},{7,8},{8,9},{9,10},{10,1... | collective-permute-start | bytes 6920 | tf_op jit(solution)/shard_map/ppermute | solution.py:17
  117.0 4.2 %collective-permute-start.7 = (f32[2,2,512]{2,1,0:T(2,128)S(1)}, f32[2,2,512]{2,1,0:T(2,128)}, u32[]{:S(2)}, u32[]{:S(2)}) collective-permute-start(f32[2,2,512]{2,1,0:T(2,128)S(1)} %bitcast.103), channel_id=1, source_target_pairs={{0,16},{16,32},{32,48},{48,64},{64,80},{80,96},{96,112},{1,17},{17... | collective-permute-start | bytes 24584 | tf_op jit(solution)/shard_map/ppermute | solution.py:23
  122.9 1.5 %copy.32 = f32[2,2,144,1]{3,2,1,0:T(8,128)} copy(f32[2,2,144,1]{2,1,0,3:T(2,128)} %bitcast.106) | data formatting | bytes 4608 | tf_op jit(solution)/shard_map/broadcast_in_dim | solution.py:55
  125.1 2.1 %fusion.7 = f32[2,2,144,512]{3,2,1,0:T(8,128)S(1)} fusion(f32[2,1,144,512]{3,2,1,0:T(8,128)S(1)} %get-tuple-element.43, f32[2,1,144,512]{3,2,1,0:T(8,128)S(1)} %get-tuple-element.44, f32[2,1,144,512]{3,2,1,0:T(8,128)S(1)} %get-tuple-element.18, f32[2,1,144,512]{3,2,1,0:T(8,128)S(1)} %get-tuple-element.17, f32[2,2,144,511]{3,2,1,0:T(8,128)S(1)} %fusion.9, ...), kind=kLoop, calls=%fused_computation.42 | loop fusion | flops 2654208 | bytes 5898816 | tf_op jit(solution)/shard_map/add | solution.py:61
  128.2 1.3 fusion.18
  (99 shorter events, 18.4 us)
Async XLA Ops:
  7.2 94.2 %all-reduce.2.cloned.1.call-start = ((), (), s32[]{:S(2)}) async-start(), calls=%async_computation | async-start | bytes 589824 | tf_op jit(solution)/shard_map/psum | solution.py:88
  8.9 1.9 %copy-start.6 = (f32[144,512]{1,0:T(8,128)S(1)}, f32[144,512]{1,0:T(8,128)}, u32[]{:S(2)}) copy-start(f32[144,512]{1,0:T(8,128)} %param.8) | copy-start | bytes 884740
  8.9 1.9 %copy-start.9 = (f32[144,512]{1,0:T(8,128)S(1)}, f32[144,512]{1,0:T(8,128)}, u32[]{:S(2)}) copy-start(f32[144,512]{1,0:T(8,128)} %param.10) | copy-start | bytes 884740
  10.9 18.4 %collective-permute-start.2 = (f32[7,512]{1,0:T(8,128)S(1)}, f32[7,512]{1,0:T(8,128)}, u32[]{:S(2)}, u32[]{:S(2)}) collective-permute-start(f32[7,512]{1,0:T(8,128)S(1)} %bitcast.99), channel_id=1, source_target_pairs={{16,0},{32,16},{48,32},{64,48},{80,64},{96,80},{112,96},{17,1},{33... | collective-permute-start | bytes 43016 | tf_op jit(solution)/shard_map/ppermute | solution.py:23
  13.3 12.4 %collective-permute-start = (f32[7,144]{1,0:T(8,128)}, f32[7,144]{1,0:T(8,128)}, u32[]{:S(2)}, u32[]{:S(2)}) collective-permute-start(f32[7,144]{1,0:T(8,128)} %slice_reduce_fusion), channel_id=1, source_target_pairs={{0,15},{1,0},{2,1},{3,2},{4,3},{5,4},{6,5},{7,6},{8,7},{9,8},{10,9... | collective-permute-start | bytes 12104 | tf_op jit(solution)/shard_map/ppermute | solution.py:17
  25.8 4.2 %copy-start.1 = (f32[7,144,511]{2,1,0:T(8,128)S(1)}, f32[7,144,511]{2,1,0:T(8,128)}, u32[]{:S(2)}) copy-start(f32[7,144,511]{2,1,0:T(8,128)} %slice.196) | copy-start | bytes 6181060
  27.6 2.4 %copy-start = (f32[7,143,512]{2,1,0:T(8,128)S(1)}, f32[7,143,512]{2,1,0:T(8,128)}, u32[]{:S(2)}) copy-start(f32[7,143,512]{2,1,0:T(8,128)} %slice.206) | copy-start | bytes 6150148
  31.5 1.1 copy-start.12
  35.1 5.4 %collective-permute-start.1 = (f32[2,2,144]{2,1,0:T(2,128)S(1)}, f32[2,2,144]{2,1,0:T(2,128)S(1)}, u32[]{:S(2)}, u32[]{:S(2)}) collective-permute-start(f32[2,2,144]{2,1,0:T(2,128)S(1)} %fusion.29), channel_id=1, source_target_pairs={{0,1},{1,2},{2,3},{3,4},{4,5},{5,6},{6,7},{7,8},{8,9},{9,10},{10,1... | collective-permute-start | bytes 6920 | tf_op jit(solution)/shard_map/ppermute | solution.py:17
  35.1 5.6 %collective-permute-start.3 = (f32[2,2,512]{2,1,0:T(2,128)S(1)}, f32[2,2,512]{2,1,0:T(2,128)S(1)}, u32[]{:S(2)}, u32[]{:S(2)}) collective-permute-start(f32[2,2,512]{2,1,0:T(2,128)S(1)} %bitcast.102), channel_id=1, source_target_pairs={{0,16},{16,32},{32,48},{48,64},{64,80},{80,96},{96,112},{1,17},{17... | collective-permute-start | bytes 24584 | tf_op jit(solution)/shard_map/ppermute | solution.py:23
  44.1 1.3 copy-start.8
  44.4 1.5 %copy-start.4 = (f32[2,2,144,512]{3,2,1,0:T(8,128)S(1)}, f32[2,2,144,512]{3,2,1,0:T(8,128)}, u32[]{:S(2)}) copy-start(f32[2,2,144,512]{3,2,1,0:T(8,128)} %param.6) | copy-start | bytes 3538948
  44.4 1.5 %copy-start.22 = (f32[2]{0:T(128)S(1)}, f32[2]{0:T(128)}, u32[]{:S(2)}) copy-start(f32[2]{0:T(128)} %get-tuple-element.47) | copy-start | bytes 28
  45.9 1.3 copy-start.7
  45.9 1.3 copy-start.10
  102.5 9.3 %copy-start.3 = (f32[144,512]{1,0:T(8,128)}, f32[144,512]{1,0:T(8,128)S(1)}, u32[]{:S(2)}) copy-start(f32[144,512]{1,0:T(8,128)S(1)} %multiply_divide_fusion) | copy-start | bytes 884740
  104.6 5.3 %collective-permute-start.4 = (f32[5,144]{1,0:T(8,128)S(1)}, f32[5,144]{1,0:T(8,128)S(1)}, u32[]{:S(2)}, u32[]{:S(2)}) collective-permute-start(f32[5,144]{1,0:T(8,128)S(1)} %fusion.25), channel_id=1, source_target_pairs={{0,15},{1,0},{2,1},{3,2},{4,3},{5,4},{6,5},{7,6},{8,7},{9,8},{10,9... | collective-permute-start | bytes 8648 | tf_op jit(solution)/shard_map/ppermute | solution.py:17
  107.3 4.5 %collective-permute-start.6 = (f32[5,512]{1,0:T(8,128)S(1)}, f32[5,512]{1,0:T(8,128)S(1)}, u32[]{:S(2)}, u32[]{:S(2)}) collective-permute-start(f32[5,512]{1,0:T(8,128)S(1)} %bitcast.100), channel_id=1, source_target_pairs={{16,0},{32,16},{48,32},{64,48},{80,64},{96,80},{112,96},{17,1},{33... | collective-permute-start | bytes 30728 | tf_op jit(solution)/shard_map/ppermute | solution.py:23
  110.0 1.7 %copy-start.2 = (f32[5,144,511]{2,1,0:T(8,128)S(1)}, f32[5,144,511]{2,1,0:T(8,128)}, u32[]{:S(2)}) copy-start(f32[5,144,511]{2,1,0:T(8,128)} %fusion.1) | copy-start | bytes 4415044
  112.1 1.2 copy-start.19
  114.6 7.7 %collective-permute-start.5 = (f32[2,2,144]{2,1,0:T(2,128)S(1)}, f32[2,2,144]{2,1,0:T(2,128)S(1)}, u32[]{:S(2)}, u32[]{:S(2)}) collective-permute-start(f32[2,2,144]{2,1,0:T(2,128)S(1)} %fusion.27), channel_id=1, source_target_pairs={{0,1},{1,2},{2,3},{3,4},{4,5},{5,6},{6,7},{7,8},{8,9},{9,10},{10,1... | collective-permute-start | bytes 6920 | tf_op jit(solution)/shard_map/ppermute | solution.py:17
  117.0 7.4 %collective-permute-start.7 = (f32[2,2,512]{2,1,0:T(2,128)S(1)}, f32[2,2,512]{2,1,0:T(2,128)}, u32[]{:S(2)}, u32[]{:S(2)}) collective-permute-start(f32[2,2,512]{2,1,0:T(2,128)S(1)} %bitcast.103), channel_id=1, source_target_pairs={{0,16},{16,32},{32,48},{48,64},{64,80},{80,96},{96,112},{1,17},{17... | collective-permute-start | bytes 24584 | tf_op jit(solution)/shard_map/ppermute | solution.py:23
  125.1 2.1 %copy-start.5 = (f32[2,2,144,512]{3,2,1,0:T(8,128)S(1)}, f32[2,2,144,512]{3,2,1,0:T(8,128)}, u32[]{:S(2)}) copy-start(f32[2,2,144,512]{3,2,1,0:T(8,128)} %get-tuple-element.7) | copy-start | bytes 3538948
  125.1 2.1 %copy-start.23 = (f32[2]{0:T(128)S(1)}, f32[2]{0:T(128)}, u32[]{:S(2)}) copy-start(f32[2]{0:T(128)} %get-tuple-element.47) | copy-start | bytes 28
  (11 other events, 10.0 us)
Sparse Core Ops, SparseCore 0:
  45.3 56.0 all-reduce.1
where the time goes:
time: 137 us; the launch traced here: 136 us
  waiting for transfers between devices  54.2 us (40%)
  other arithmetic  30.5 us (22%)
  starting transfers between devices  23 us (17%)
  between operations  14.5 us (11%)
  local copies, waits for them, and re-layouts  14.2 us (10%)
    psum x1, waiting for transfers between devices, compute_friction(): variance_total = lax.psum(variance_local, 'cons')  52.7 us
    ppermute x4, starting transfers between devices, passed_along(): return lax.ppermute(value, axis, pairs)  12 us
    ppermute x4, starting transfers between devices, passed_along_2(): return lax.ppermute(block, axis, route)  11 us
    unnamed x56, local copies, waits for them, and re-layouts  4.38 us
    mul x1, other arithmetic, finish(): cu = 0.5 * (trans_u + west_u)  3.39 us
    concatenate x2, other arithmetic, forward_rims(): jnp.concatenate([planes[:, :, 1:], east_col[:, :, None]], axis=2)  3.17 us
  transfers between devices with their start and end apart: 9, of which 3 were waited for; matrix products, arithmetic and copies ran while one was open for 13% of the time, Pallas kernels for 0%

commit v1 on v0

--- a/solution.py
+++ b/solution.py
@@ -85,7 +85,7 @@
 
 
 def compute_friction(variance_local, depth):
-    variance_total = lax.psum(variance_local, "cons")
+    variance_total = jnp.sum(lax.all_gather(variance_local, "cons"), axis=0)
     return DRAG * jnp.sqrt(variance_total + BACKGROUND) / depth
 
 

time: 137 us -> 121 us (0.88)
  waiting for transfers between devices: 54.2 us -> 39.2 us
  starting transfers between devices: 23 us -> 21.3 us
    psum x1 -> x0, waiting for transfers between devices: 52.7 us -> none  [compute_friction(): variance_total = lax.psum(variance_local, 'cons')]
    all_gather x0 -> x1, waiting for transfers between devices: none -> 37.8 us  [compute_friction(): variance_total = jnp.sum(lax.all_gather(variance_local, 'cons'), axis=0)]
    ppermute x4, starting transfers between devices: 12 us -> 9.95 us  [passed_along(): return lax.ppermute(value, axis, pairs)]
    reduce_sum x0 -> x1, other arithmetic: none -> 1.4 us  [compute_friction(): variance_total = jnp.sum(lax.all_gather(variance_local, 'cons'), axis=0)]
  transfers between devices with their start and end apart: 9 -> 9, of which waited for: 3 -> 3; matrix products, arithmetic and copies ran while one was open for 13% -> 15% of each run, Pallas kernels for 0% -> 0%
where the time goes in v1:
time: 121 us; the launch traced here: 120 us
  waiting for transfers between devices  39.2 us (32%)
  other arithmetic  30.9 us (26%)
  starting transfers between devices  21.3 us (18%)
  between operations  14.5 us (12%)
  local copies, waits for them, and re-layouts  14.1 us (12%)
    all_gather x1, waiting for transfers between devices, compute_friction(): variance_total = jnp.sum(lax.all_gather(variance_local, 'cons'), axis=0)  37.8 us
    ppermute x4, starting transfers between devices, passed_along_2(): return lax.ppermute(block, axis, route)  11.3 us
    ppermute x4, starting transfers between devices, passed_along(): return lax.ppermute(value, axis, pairs)  9.95 us
    unnamed x56, local copies, waits for them, and re-layouts  4.37 us
    mul x1, other arithmetic, finish(): cu = 0.5 * (trans_u + west_u)  3.39 us
    concatenate x2, other arithmetic, forward_rims(): jnp.concatenate([planes[:, :, 1:], east_col[:, :, None]], axis=2)  3.17 us
  transfers between devices with their start and end apart: 9, of which 3 were waited for; matrix products, arithmetic and copies ran while one was open for 15% of the time, Pallas kernels for 0%

profile of v1, /device:TPU:1, one launch (start us, length us, event | category | flops | bytes accessed | tf_op | source)
XLA Modules:
  0.0 120.1 jit_solution(137248660780644397)
XLA Ops:
  7.2 1.7 %fusion.62 = (f32[144,512]{1,0:T(8,128)}, f32[1,144,512]{2,1,0:T(8,128)S(1)}) fusion(s32[144,512]{1,0:T(8,128)} %param.9), kind=kLoop, calls=%fused_computation.150 | loop fusion | flops 73728 | bytes 884736 | tf_op jit(solution)/shard_map/convert_element_type | solution.py:100
  8.9 1.9 %sub.52 = f32[2,2,144,512]{3,2,1,0:T(8,128)S(1)} subtract(f32[2,2,144,512]{3,2,1,0:T(8,128)} %param.6, f32[2,2,144,512]{3,2,1,0:T(8,128)} %param.7) | non-fusion elementwise | flops 294912 | bytes 3538944 | tf_op jit(solution)/shard_map/sub | solution.py:102
  10.9 1.3 %collective-permute-start.2 = (f32[7,512]{1,0:T(8,128)S(1)}, f32[7,512]{1,0:T(8,128)}, u32[]{:S(2)}, u32[]{:S(2)}) collective-permute-start(f32[7,512]{1,0:T(8,128)S(1)} %bitcast.101), channel_id=1, source_target_pairs={{16,0},{32,16},{48,32},{64,48},{80,64},{96,80},{112,96},{17,1},{33... | collective-permute-start | bytes 43016 | tf_op jit(solution)/shard_map/ppermute | solution.py:23
  13.3 6.9 %collective-permute-start = (f32[7,144]{1,0:T(8,128)}, f32[7,144]{1,0:T(8,128)}, u32[]{:S(2)}, u32[]{:S(2)}) collective-permute-start(f32[7,144]{1,0:T(8,128)} %slice_reduce_fusion), channel_id=1, source_target_pairs={{0,15},{1,0},{2,1},{3,2},{4,3},{5,4},{6,5},{7,6},{8,7},{9,8},{10,9... | collective-permute-start | bytes 12104 | tf_op jit(solution)/shard_map/ppermute | solution.py:17
  20.2 1.3 %dynamic-slice_negate_fusion = (f32[2]{0:T(128)}, f32[2]{0:T(128)}, f32[2]{0:T(128)}) fusion(f32[8]{0:T(128)} %constant.41.clone, s32[]{:T(128)S(6)} %select_n.3), kind=kLoop, calls=%fused_computation.144 | loop fusion | flops 4 | bytes 36 | tf_op jit(solution)/shard_map/neg | solution.py:62
  22.1 1.8 %slice.206 = f32[7,143,512]{2,1,0:T(8,128)} slice(f32[7,144,512]{2,1,0:T(8,128)S(1)} %pad_maximum_fusion), slice={[0:7], [1:144], [0:512]} | slice | bytes 4100096 | tf_op jit(solution)/shard_map/slice | solution.py:48
  23.9 1.9 %slice.196 = f32[7,144,511]{2,1,0:T(8,128)} slice(f32[7,144,512]{2,1,0:T(8,128)S(1)} %pad_maximum_fusion), slice={[0:7], [0:144], [1:512]} | slice | bytes 4120704 | tf_op jit(solution)/shard_map/slice | solution.py:47
  25.8 1.9 %copy.28 = f32[7,144,1]{2,1,0:T(8,128)} copy(f32[7,144,1]{1,0,2:T(8,128)} %bitcast.4) | data formatting | bytes 8064 | tf_op jit(solution)/shard_map/broadcast_in_dim | solution.py:47
  27.6 1.6 %fusion.14 = f32[4,144,512]{2,1,0:T(8,128)S(1)} fusion(f32[7,144,511]{2,1,0:T(8,128)} %slice.196, f32[7,144,1]{2,1,0:T(8,128)} %copy.28), kind=kLoop, calls=%fused_computation.49 | loop fusion | flops 294912 | bytes 3244032 | tf_op jit(solution)/shard_map/concatenate | solution.py:47
  30.0 1.5 %fusion.60 = (f32[144,512]{1,0:T(8,128)S(1)}, f32[144,512]{1,0:T(8,128)S(1)}, f32[144,512]{1,0:T(8,128)S(1)}, f32[144,512]{1,0:T(8,128)S(1)}, f32[144,512]{1,0:T...) fusion(f32[144,512]{1,0:T(8,128)} %param.10, ...), kind=kLoop, calls=%fused_computation.149 | loop fusion | flops 1548288 | bytes 7372800 | tf_op jit(solution)/shard_map/mul | solution.py:32
  35.1 4.3 %collective-permute-start.3 = (f32[2,2,512]{2,1,0:T(2,128)S(1)}, f32[2,2,512]{2,1,0:T(2,128)S(1)}, u32[]{:S(2)}, u32[]{:S(2)}) collective-permute-start(f32[2,2,512]{2,1,0:T(2,128)S(1)} %bitcast.104), channel_id=1, source_target_pairs={{0,16},{16,32},{32,48},{48,64},{64,80},{80,96},{96,112},{1,17},{17... | collective-permute-start | bytes 24584 | tf_op jit(solution)/shard_map/ppermute | solution.py:23
  39.4 1.1 fusion.8
  40.7 3.4 %add_multiply_fusion.1 = (f32[2,2,144,512]{3,2,1,0:T(8,128)S(1)}, f32[2,2,144,512]{3,2,1,0:T(8,128)}, f32[2,2,144,512]{3,2,1,0:T(8,128)S(1)}) fusion(f32[2,1,144,512]{3,2,1,0:T(8,128)S(1)} %get-tuple-element.22, f32[2,1,144,512]{3,2,1,0:T(8,128)S(1)} %get-tuple-element.21, f32[2,2,144,511]{3,2,1,0:T(8,128)} %fusion.12, f32[2,2,144,1]{3,2,1,0:T(8,128)S(1)} %copy.29, ...), kind=kLoop, calls=%fused_computation.61 | loop fusion | flops 3833856 | bytes 8258112 | tf_op jit(solution)/shard_map/mul | solution.py:64
  47.2 1.5 %fusion.56 = (f32[2,2,144,512]{3,2,1,0:T(8,128)S(1)}, f32[2,2,144,512]{3,2,1,0:T(8,128)}) fusion(f32[2,2,144,512]{3,2,1,0:T(8,128)S(1)} %copy-done.7, f32[2,2,144,512]{3,2,1,0:T(8,128)S(1)} %copy-done.4, f32[2,1,144,512]{3,2,1,0:T(8,128)S(1)} %get-tuple-element.28, f32[2,1,144,512]{3,2,1,0:T(8,128)S(1)} %get-tuple-element.27, f32[144,512]{1,0:T(8,128)S(1)} %copy-done.10), kind=kLoop, calls=%fused_computation.147 | loop fusion | flops 1474560 | bytes 6193152 | tf_op jit(solution)/shard_map/sub | solution.py:138
  48.7 37.8 %all-gather.3.cloned.1.call-done = f32[576,512]{1,0:T(8,128)} async-done(((f32[144,512]{1,0:T(8,128)}), f32[576,512]{1,0:T(8,128)}) %all-gather.3.cloned.1.call-update) | async-done | bytes 1179664 | tf_op jit(solution)/shard_map/all_gather | solution.py:88
  86.5 1.4 %reduce_sum.19 = f32[144,512]{1,0:T(8,128)S(1)} reduce(f32[4,144,512]{2,1,0:T(8,128)} %bitcast.100, f32[]{:T(128)} %constant.14.clone.1), dimensions={0}, to_apply=%region_1.0 | reduce | flops 221184 | bytes 1474564 | tf_op jit(solution)/shard_map/reduce_sum | solution.py:88
  88.3 1.6 %fusion.1 = f32[5,144,511]{2,1,0:T(8,128)} fusion(f32[4,144,512]{2,1,0:T(8,128)S(1)} %bitcast.83, f32[1,144,512]{2,1,0:T(8,128)S(1)} %bitcast.89), kind=kLoop, calls=%fused_computation.32 | loop fusion | flops 367920 | bytes 2946240 | tf_op jit(solution)/shard_map/concatenate | solution.py:139
  91.0 1.3 %collective-permute-start.6 = (f32[5,512]{1,0:T(8,128)S(1)}, f32[5,512]{1,0:T(8,128)S(1)}, u32[]{:S(2)}, u32[]{:S(2)}) collective-permute-start(f32[5,512]{1,0:T(8,128)S(1)} %bitcast.102), channel_id=1, source_target_pairs={{16,0},{32,16},{48,32},{64,48},{80,64},{96,80},{112,96},{17,1},{33... | collective-permute-start | bytes 30728 | tf_op jit(solution)/shard_map/ppermute | solution.py:23
  93.5 1.5 %fusion.3 = f32[4,144,512]{2,1,0:T(8,128)S(1)} fusion(f32[5,144,511]{2,1,0:T(8,128)} %fusion.1, f32[5,144,1]{2,1,0:T(8,128)S(1)} %copy.31), kind=kLoop, calls=%fused_computation.38 | loop fusion | flops 294912 | bytes 2654208 | tf_op jit(solution)/shard_map/concatenate | solution.py:47
  98.3 2.2 %collective-permute-start.5 = (f32[2,2,144]{2,1,0:T(2,128)S(1)}, f32[2,2,144]{2,1,0:T(2,128)S(1)}, u32[]{:S(2)}, u32[]{:S(2)}) collective-permute-start(f32[2,2,144]{2,1,0:T(2,128)S(1)} %fusion.27), channel_id=1, source_target_pairs={{0,1},{1,2},{2,3},{3,4},{4,5},{5,6},{6,7},{7,8},{8,9},{9,10},{10,1... | collective-permute-start | bytes 6920 | tf_op jit(solution)/shard_map/ppermute | solution.py:17
  100.5 4.4 %collective-permute-start.7 = (f32[2,2,512]{2,1,0:T(2,128)S(1)}, f32[2,2,512]{2,1,0:T(2,128)}, u32[]{:S(2)}, u32[]{:S(2)}) collective-permute-start(f32[2,2,512]{2,1,0:T(2,128)S(1)} %bitcast.105), channel_id=1, source_target_pairs={{0,16},{16,32},{32,48},{48,64},{64,80},{80,96},{96,112},{1,17},{17... | collective-permute-start | bytes 24584 | tf_op jit(solution)/shard_map/ppermute | solution.py:23
  106.6 1.5 %copy.32 = f32[2,2,144,1]{3,2,1,0:T(8,128)} copy(f32[2,2,144,1]{2,1,0,3:T(2,128)} %bitcast.108) | data formatting | bytes 4608 | tf_op jit(solution)/shard_map/broadcast_in_dim | solution.py:55
  108.9 2.1 %fusion.7 = f32[2,2,144,512]{3,2,1,0:T(8,128)S(1)} fusion(f32[2,1,144,512]{3,2,1,0:T(8,128)S(1)} %get-tuple-element.43, f32[2,1,144,512]{3,2,1,0:T(8,128)S(1)} %get-tuple-element.44, f32[2,1,144,512]{3,2,1,0:T(8,128)S(1)} %get-tuple-element.18, f32[2,1,144,512]{3,2,1,0:T(8,128)S(1)} %get-tuple-element.17, f32[2,2,144,511]{3,2,1,0:T(8,128)S(1)} %fusion.9, ...), kind=kLoop, calls=%fused_computation.42 | loop fusion | flops 2654208 | bytes 5898816 | tf_op jit(solution)/shard_map/add | solution.py:61
  111.9 1.3 %fusion.18 = f32[2,2,144,512]{3,2,1,0:T(8,128)} fusion(f32[2,2,144,512]{3,2,1,0:T(8,128)S(1)} %copy-done.5, f32[2,1,144,512]{3,2,1,0:T(8,128)S(1)} %get-tuple-element.26, f32[2,1,144,512]{3,2,1,0:T(8,128)S(1)} %get-tuple-element.25, f32[144,512]{1,0:T(8,128)S(1)} %copy-done.11), kind=kLoop, calls=%fused_computation.57 | loop fusion | flops 1179648 | bytes 3833856 | tf_op jit(solution)/shard_map/mul | solution.py:63
  (100 shorter events, 18.4 us)
Async XLA Ops:
  7.2 79.3 %all-gather.3.cloned.1.call-start = ((), (), s32[]{:S(2)}) async-start(), calls=%async_computation | async-start | bytes 1474560 | tf_op jit(solution)/shard_map/all_gather | solution.py:88
  8.9 1.9 %copy-start.6 = (f32[144,512]{1,0:T(8,128)S(1)}, f32[144,512]{1,0:T(8,128)}, u32[]{:S(2)}) copy-start(f32[144,512]{1,0:T(8,128)} %param.8) | copy-start | bytes 884740
  8.9 1.9 %copy-start.9 = (f32[144,512]{1,0:T(8,128)S(1)}, f32[144,512]{1,0:T(8,128)}, u32[]{:S(2)}) copy-start(f32[144,512]{1,0:T(8,128)} %param.10) | copy-start | bytes 884740
  10.9 18.4 %collective-permute-start.2 = (f32[7,512]{1,0:T(8,128)S(1)}, f32[7,512]{1,0:T(8,128)}, u32[]{:S(2)}, u32[]{:S(2)}) collective-permute-start(f32[7,512]{1,0:T(8,128)S(1)} %bitcast.101), channel_id=1, source_target_pairs={{16,0},{32,16},{48,32},{64,48},{80,64},{96,80},{112,96},{17,1},{33... | collective-permute-start | bytes 43016 | tf_op jit(solution)/shard_map/ppermute | solution.py:23
  13.3 12.4 %collective-permute-start = (f32[7,144]{1,0:T(8,128)}, f32[7,144]{1,0:T(8,128)}, u32[]{:S(2)}, u32[]{:S(2)}) collective-permute-start(f32[7,144]{1,0:T(8,128)} %slice_reduce_fusion), channel_id=1, source_target_pairs={{0,15},{1,0},{2,1},{3,2},{4,3},{5,4},{6,5},{7,6},{8,7},{9,8},{10,9... | collective-permute-start | bytes 12104 | tf_op jit(solution)/shard_map/ppermute | solution.py:17
  25.8 4.2 %copy-start.1 = (f32[7,144,511]{2,1,0:T(8,128)S(1)}, f32[7,144,511]{2,1,0:T(8,128)}, u32[]{:S(2)}) copy-start(f32[7,144,511]{2,1,0:T(8,128)} %slice.196) | copy-start | bytes 6181060
  27.6 2.4 %copy-start = (f32[7,143,512]{2,1,0:T(8,128)S(1)}, f32[7,143,512]{2,1,0:T(8,128)}, u32[]{:S(2)}) copy-start(f32[7,143,512]{2,1,0:T(8,128)} %slice.206) | copy-start | bytes 6150148
  31.5 1.1 copy-start.12
  35.1 5.4 %collective-permute-start.1 = (f32[2,2,144]{2,1,0:T(2,128)S(1)}, f32[2,2,144]{2,1,0:T(2,128)S(1)}, u32[]{:S(2)}, u32[]{:S(2)}) collective-permute-start(f32[2,2,144]{2,1,0:T(2,128)S(1)} %fusion.29), channel_id=1, source_target_pairs={{0,1},{1,2},{2,3},{3,4},{4,5},{5,6},{6,7},{7,8},{8,9},{9,10},{10,1... | collective-permute-start | bytes 6920 | tf_op jit(solution)/shard_map/ppermute | solution.py:17
  35.1 5.6 %collective-permute-start.3 = (f32[2,2,512]{2,1,0:T(2,128)S(1)}, f32[2,2,512]{2,1,0:T(2,128)S(1)}, u32[]{:S(2)}, u32[]{:S(2)}) collective-permute-start(f32[2,2,512]{2,1,0:T(2,128)S(1)} %bitcast.104), channel_id=1, source_target_pairs={{0,16},{16,32},{32,48},{48,64},{64,80},{80,96},{96,112},{1,17},{17... | collective-permute-start | bytes 24584 | tf_op jit(solution)/shard_map/ppermute | solution.py:23
  44.1 1.3 %copy-start.8 = (f32[2,2,144,512]{3,2,1,0:T(8,128)S(1)}, f32[2,2,144,512]{3,2,1,0:T(8,128)}, u32[]{:S(2)}) copy-start(f32[2,2,144,512]{3,2,1,0:T(8,128)} %get-tuple-element.13) | copy-start | bytes 3538948
  44.4 1.5 %copy-start.4 = (f32[2,2,144,512]{3,2,1,0:T(8,128)S(1)}, f32[2,2,144,512]{3,2,1,0:T(8,128)}, u32[]{:S(2)}) copy-start(f32[2,2,144,512]{3,2,1,0:T(8,128)} %param.6) | copy-start | bytes 3538948
  44.4 1.5 %copy-start.22 = (f32[2]{0:T(128)S(1)}, f32[2]{0:T(128)}, u32[]{:S(2)}) copy-start(f32[2]{0:T(128)} %get-tuple-element.47) | copy-start | bytes 28
  45.9 1.3 %copy-start.7 = (f32[2,2,144,512]{3,2,1,0:T(8,128)S(1)}, f32[2,2,144,512]{3,2,1,0:T(8,128)}, u32[]{:S(2)}) copy-start(f32[2,2,144,512]{3,2,1,0:T(8,128)} %param.7) | copy-start | bytes 3538948
  45.9 1.3 %copy-start.10 = (f32[144,512]{1,0:T(8,128)S(1)}, f32[144,512]{1,0:T(8,128)}, u32[]{:S(2)}) copy-start(f32[144,512]{1,0:T(8,128)} %get-tuple-element.41) | copy-start | bytes 884740
  88.0 7.5 %copy-start.3 = (f32[144,512]{1,0:T(8,128)}, f32[144,512]{1,0:T(8,128)S(1)}, u32[]{:S(2)}) copy-start(f32[144,512]{1,0:T(8,128)S(1)} %multiply_divide_fusion) | copy-start | bytes 884740
  90.1 3.2 %collective-permute-start.4 = (f32[5,144]{1,0:T(8,128)S(1)}, f32[5,144]{1,0:T(8,128)S(1)}, u32[]{:S(2)}, u32[]{:S(2)}) collective-permute-start(f32[5,144]{1,0:T(8,128)S(1)} %fusion.25), channel_id=1, source_target_pairs={{0,15},{1,0},{2,1},{3,2},{4,3},{5,4},{6,5},{7,6},{8,7},{9,8},{10,9... | collective-permute-start | bytes 8648 | tf_op jit(solution)/shard_map/ppermute | solution.py:17
  91.0 4.5 %collective-permute-start.6 = (f32[5,512]{1,0:T(8,128)S(1)}, f32[5,512]{1,0:T(8,128)S(1)}, u32[]{:S(2)}, u32[]{:S(2)}) collective-permute-start(f32[5,512]{1,0:T(8,128)S(1)} %bitcast.102), channel_id=1, source_target_pairs={{16,0},{32,16},{48,32},{64,48},{80,64},{96,80},{112,96},{17,1},{33... | collective-permute-start | bytes 30728 | tf_op jit(solution)/shard_map/ppermute | solution.py:23
  93.5 2.0 %copy-start.2 = (f32[5,144,511]{2,1,0:T(8,128)S(1)}, f32[5,144,511]{2,1,0:T(8,128)}, u32[]{:S(2)}) copy-start(f32[5,144,511]{2,1,0:T(8,128)} %fusion.1) | copy-start | bytes 4415044
  95.8 1.2 %copy-start.19 = (f32[144,512]{1,0:T(8,128)S(1)}, f32[144,512]{1,0:T(8,128)}, u32[]{:S(2)}) copy-start(f32[144,512]{1,0:T(8,128)} %copy-done.18) | copy-start | bytes 884740
  98.3 7.7 %collective-permute-start.5 = (f32[2,2,144]{2,1,0:T(2,128)S(1)}, f32[2,2,144]{2,1,0:T(2,128)S(1)}, u32[]{:S(2)}, u32[]{:S(2)}) collective-permute-start(f32[2,2,144]{2,1,0:T(2,128)S(1)} %fusion.27), channel_id=1, source_target_pairs={{0,1},{1,2},{2,3},{3,4},{4,5},{5,6},{6,7},{7,8},{8,9},{9,10},{10,1... | collective-permute-start | bytes 6920 | tf_op jit(solution)/shard_map/ppermute | solution.py:17
  100.5 7.7 %collective-permute-start.7 = (f32[2,2,512]{2,1,0:T(2,128)S(1)}, f32[2,2,512]{2,1,0:T(2,128)}, u32[]{:S(2)}, u32[]{:S(2)}) collective-permute-start(f32[2,2,512]{2,1,0:T(2,128)S(1)} %bitcast.105), channel_id=1, source_target_pairs={{0,16},{16,32},{32,48},{48,64},{64,80},{80,96},{96,112},{1,17},{17... | collective-permute-start | bytes 24584 | tf_op jit(solution)/shard_map/ppermute | solution.py:23
  108.9 2.1 %copy-start.5 = (f32[2,2,144,512]{3,2,1,0:T(8,128)S(1)}, f32[2,2,144,512]{3,2,1,0:T(8,128)}, u32[]{:S(2)}) copy-start(f32[2,2,144,512]{3,2,1,0:T(8,128)} %get-tuple-element.7) | copy-start | bytes 3538948
  108.9 2.1 %copy-start.23 = (f32[2]{0:T(128)S(1)}, f32[2]{0:T(128)}, u32[]{:S(2)}) copy-start(f32[2]{0:T(128)} %get-tuple-element.47) | copy-start | bytes 28
  (11 other events, 10.0 us)
Sparse Core Ops, SparseCore 0:
  45.3 41.1 all-gather.2
